TPU v7x, 32 devices: a whole 2x2x4 slice. The times are simulated.
32 devices in a mesh: row: 4 (over z), replica: 4 (over y, core), feat: 2 (over x).
Axes of the slice: x: 2, y: 2, z: 4, core: 2. Of those that a mesh axis runs over, the one named last changes fastest.
Arguments:
- features: bfloat16 [4, 4096, 256], P('replica', ('row', 'feat')), may hold values from -6 to 6
- tiles: bfloat16 [4, 32, 4, 3, 128, 128], P('replica', ('row', 'feat')), may hold values from 0 to 1
- block_cols: int32 [4, 32, 4, 3], P('replica', ('row', 'feat')), may hold values from 0 to 7
- block_counts: int32 [4, 32, 4], P('replica', ('row', 'feat')), may hold values from 0 to 3, as said below
- degrees: int32 [4, 4096], P('replica', ('row', 'feat')), may hold values from 32 to 287
- w_self: bfloat16 [256, 256], P(None, 'feat'), may hold values from -0.375 to 0.375
- w_neigh: bfloat16 [256, 256], P(None, 'feat'), may hold values from -0.375 to 0.375
- gamma: float32 [256], P('feat'), may hold values from 0.5 to 1.5
- beta: float32 [256], P('feat'), may hold values from -3 to 3
Outputs:
- hidden_out: bfloat16 [4, 4096, 256], P('replica', 'row', 'feat')
Inputs may be any that keep to these rules, and one draw needn't show every extreme that they name: `block_counts`: some block row uses all 3 slots of some source shard in every partition.
All inputs are finite; a program needn't handle non-finite values.
Results may differ from a plain program's by a relative error of at most 0.001.
Values may be sent and summed in bfloat16 or wider, within the bound.
No kernel may reach another device: no remote copies, remote signals or barrier semaphores. Data moves between devices by JAX's collectives and lax.ppermute only.
A program may use at most 128 MiB of HBM per device.

v0:
```python
import jax
import jax.numpy as jnp
from jax import lax
from jax.sharding import PartitionSpec as P


def per_device(features, tiles, block_cols, block_counts, degrees, w_self, w_neigh, gamma, beta):
    local_x = features[0]
    local_tiles = tiles[0]
    local_cols = block_cols[0]
    local_counts = block_counts[0]
    nodes_here = local_x.shape[0]
    width = local_x.shape[1]
    block_size = local_tiles.shape[3]
    slots = local_tiles.shape[2]
    row_blocks = local_tiles.shape[0]
    pair = lax.all_gather(local_x, "feat", axis=0, tiled=True)
    shard_rows = pair.shape[0]
    shard_blocks = shard_rows // block_size
    slot_index = jnp.arange(slots, dtype=jnp.int32)[None, :]
    start_total = jnp.zeros((row_blocks, block_size, width), jnp.float32)
    piece = lax.all_gather(pair, "row", axis=0, tiled=True)
    count_shards = piece.shape[0] // shard_rows
    shards = piece.reshape(count_shards, shard_blocks, block_size, width)

    def one_shard(step, acc):
        shard = lax.dynamic_index_in_dim(shards, step, 0, keepdims=False)
        counts_now = lax.dynamic_index_in_dim(local_counts, step, 1, keepdims=False)
        cols_now = lax.dynamic_index_in_dim(local_cols, step, 1, keepdims=False)
        tiles_now = lax.dynamic_index_in_dim(local_tiles, step, 1, keepdims=False)
        picked = shard[cols_now]
        used = slot_index < counts_now[:, None]
        masked = jnp.where(used[:, :, None, None], tiles_now, jnp.zeros((), tiles_now.dtype))
        return acc + jnp.einsum(
            "bcij,bcjf->bif", masked, picked, preferred_element_type=jnp.float32
        )

    agg_sum = lax.fori_loop(0, count_shards, one_shard, start_total).reshape(nodes_here, width)
    agg = (agg_sum / degrees[0][:, None].astype(jnp.float32)).astype(jnp.bfloat16)
    agg_pair = lax.all_gather(agg, "feat", axis=0, tiled=True)
    pre = jnp.dot(pair, w_self, preferred_element_type=jnp.float32) + jnp.dot(
        agg_pair, w_neigh, preferred_element_type=jnp.float32
    )
    col_sum, col_sq = lax.psum(
        (jnp.sum(pre, axis=0), jnp.sum(pre * pre, axis=0)), ("row", "replica")
    )
    total_nodes = pre.shape[0] * lax.axis_size("row") * lax.axis_size("replica")
    mean = col_sum / total_nodes
    var = col_sq / total_nodes - mean * mean
    normed = gamma * (pre - mean) / jnp.sqrt(var + 1e-05) + beta
    return jnp.maximum(normed, 0.0).astype(jnp.bfloat16)[None]


def solution(mesh):
    in_specs = (
        P("replica", ("row", "feat"), None),
        P("replica", ("row", "feat"), None, None, None, None),
        P("replica", ("row", "feat"), None, None),
        P("replica", ("row", "feat"), None),
        P("replica", ("row", "feat")),
        P(None, "feat"),
        P(None, "feat"),
        P("feat"),
        P("feat"),
    )
    out_specs = P("replica", "row", "feat")
    return jax.shard_map(
        per_device, mesh=mesh, in_specs=in_specs, out_specs=out_specs, check_vma=False
    )
```

profile of v0, /device:TPU:0, one launch (start us, length us, event | category | flops | bytes accessed | tf_op | source)
XLA Modules:
  0.0 121.8 jit_solution(17375432722191585981)
XLA Ops:
  6.5 0.0 copy-start
  6.5 0.0 all-gather.4.cloned.1.call-start
  6.5 12.0 %all-gather = bf16[1,1024,256]{2,1,0:T(8,128)(2,1)} all-gather(bf16[1,512,256]{2,1,0:T(8,128)(2,1)} %param.11), channel_id=2, replica_groups=mesh['row'=4,'replica'=4,'feat'=2] {'feat'}, dimensions={1}, use_global_device_ids=true | all-gather | bytes 786432 | tf_op jit(solution)/shard_map/all_gather | solution.py:17
  18.6 0.0 all-gather.4.cloned.1.call-update
  18.6 0.0 copy-start.4
  18.6 0.0 copy-start.5
  18.6 0.0 copy-start.6
  18.6 0.0 copy-start.1
  18.7 0.0 copy-start.3
  18.7 1.6 %copy.20 = bf16[1,4,4,3,128,128]{5,4,3,1,2,0:T(8,128)(2,1)S(1)} copy(bf16[1,4,4,3,128,128]{5,4,3,2,1,0:T(8,128)(2,1)} %param.12) | data formatting | bytes 3145728 | tf_op args[1]
  20.2 0.0 copy-done.4
  20.3 0.1 copy.17
  20.4 0.0 copy-done.5
  20.4 0.1 copy.16
  20.5 0.0 copy-done.6
  20.5 0.0 copy-done.1
  20.5 0.0 copy-done.3
  20.5 1.1 fusion.10
  21.6 43.2 %all-gather.4.cloned.1.call-done = bf16[1,4096,256]{2,1,0:T(8,128)(2,1)} async-done(((bf16[1,1024,256]{2,1,0:T(8,128)(2,1)}), bf16[1,4096,256]{2,1,0:T(8,128)(2,1)}) %all-gather.4.cloned.1.call-update) | async-done | bytes 2097168 | tf_op jit(solution)/shard_map/all_gather | solution.py:22
  64.7 9.8 %while.14 = (s32[]{:T(128)}, f32[4,128,256]{2,1,0:T(8,128)S(1)}, s32[4,4]{0,1:T(4,128)S(1)}, bf16[4,4,3,128,128]{4,3,2,0,1:T(8,128)(2,1)S(1)}, bf16[4,8,128,256]...) while((s32[]{:T(128)}, f32[4,128,256]{2,1,0:T(8,128)S(1)}, ...), condition=%wide.region_1.2_spmd.clone, body=%wide.region_0.1_spmd.clone.sunk | while | flops 101123120 | bytes 4854827 | solution.py:38
  64.7 1.1 dynamic-slice_bitcast_fusion.2
  65.8 0.1 copy.22
  65.9 0.1 reshape.106
  66.0 0.6 gather_fusion
  66.6 0.1 iota_compare_fusion.2
  66.7 0.4 fusion.23
  67.2 1.1 dynamic-slice_bitcast_fusion.2
  68.3 0.1 copy.22
  68.4 0.1 reshape.106
  68.5 0.6 gather_fusion
  69.1 0.1 iota_compare_fusion.2
  69.2 0.4 fusion.23
  69.6 1.1 dynamic-slice_bitcast_fusion.2
  70.7 0.1 copy.22
  70.8 0.1 reshape.106
  70.9 0.6 gather_fusion
  71.5 0.1 iota_compare_fusion.2
  71.6 0.4 fusion.23
  72.1 1.1 dynamic-slice_bitcast_fusion.2
  73.2 0.1 copy.22
  73.2 0.1 reshape.106
  73.3 0.6 gather_fusion
  74.0 0.1 iota_compare_fusion.2
  74.0 0.4 fusion.23
  74.5 0.0 copy-start.2
  74.5 0.0 copy-start.7
  74.5 0.0 copy-start.8
  74.5 0.1 fusion.9
  74.7 8.6 %all_gather.11 = bf16[1024,256]{1,0:T(8,128)(2,1)S(1)} all-gather(bf16[512,256]{1,0:T(8,128)(2,1)S(1)} %fusion.9), channel_id=1, replica_groups=mesh['row'=4,'replica'=4,'feat'=2] {'feat'}, dimensions={0}, use_global_device_ids=true | all-gather | bytes 786432 | tf_op jit(solution)/shard_map/all_gather | solution.py:40
  83.2 0.0 copy-done
  83.2 0.0 copy-done.2
  83.2 0.4 fusion.13
  83.6 30.5 %all-reduce = (f32[128]{0:T(128)S(1)}, f32[128]{0:T(128)S(1)}) all-reduce(f32[128]{0:T(128)S(1)} %get-tuple-element.166, f32[128]{0:T(128)S(1)} %get-tuple-element.165), channel_id=1, replica_groups=mesh['row'=4,'replica'=4,'feat'=2] {'row','replica'}, use_global_device_ids=true, to_apply=%region_5.6 | all-reduce | flops 256 | bytes 2048 | tf_op jit(solution)/shard_map/psum | solution.py:44
  114.2 0.0 copy-done.7
  114.2 0.0 copy-done.8
  114.2 0.8 fusion.12
  (15 shorter events, 0.1 us)
Async XLA Ops:
  6.5 76.7 %copy-start = (bf16[256,128]{1,0:T(8,128)(2,1)S(1)}, bf16[256,128]{1,0:T(8,128)(2,1)}, u32[]{:S(2)}) copy-start(bf16[256,128]{1,0:T(8,128)(2,1)} %param.17) | copy-start | bytes 196612
  6.5 58.2 %all-gather.4.cloned.1.call-start = ((), (), s32[]{:S(2)}) async-start(), calls=%async_computation | async-start | bytes 2621440 | tf_op jit(solution)/shard_map/all_gather | solution.py:22
  18.6 1.6 %copy-start.4 = (s32[1,4,4,3]{2,1,3,0:T(4,128)S(1)}, s32[1,4,4,3]{2,1,3,0:T(4,128)}, u32[]{:S(2)}) copy-start(s32[1,4,4,3]{2,1,3,0:T(4,128)} %param.13) | copy-start | bytes 580
  18.6 1.7 %copy-start.5 = (s32[1,4,4]{2,1,0:T(4,128)S(1)}, s32[1,4,4]{2,1,0:T(4,128)}, u32[]{:S(2)}) copy-start(s32[1,4,4]{2,1,0:T(4,128)} %param.14) | copy-start | bytes 196
  18.6 1.8 %copy-start.6 = (s32[1,512]{1,0:T(1,128)S(1)}, s32[1,512]{1,0:T(1,128)}, u32[]{:S(2)}) copy-start(s32[1,512]{1,0:T(1,128)} %param.15) | copy-start | bytes 6148
  18.6 1.8 %copy-start.1 = (bf16[1,1024,256]{2,1,0:T(8,128)(2,1)S(1)}, bf16[1,1024,256]{2,1,0:T(8,128)(2,1)}, u32[]{:S(2)}) copy-start(bf16[1,1024,256]{2,1,0:T(8,128)(2,1)} %all-gather) | copy-start | bytes 1572868
  18.7 1.8 %copy-start.3 = (bf16[256,128]{1,0:T(8,128)(2,1)S(1)}, bf16[256,128]{1,0:T(8,128)(2,1)}, u32[]{:S(2)}) copy-start(bf16[256,128]{1,0:T(8,128)(2,1)} %param.16) | copy-start | bytes 196612
  74.5 8.7 %copy-start.2 = (f32[1024,128]{1,0:T(8,128)S(1)}, f32[1024,128]{1,0:T(8,128)}, u32[]{:S(2)}) copy-start(f32[1024,128]{1,0:T(8,128)} %fusion.10) | copy-start | bytes 1572868
  74.5 39.7 %copy-start.7 = (f32[128]{0:T(128)S(1)}, f32[128]{0:T(128)}, u32[]{:S(2)}) copy-start(f32[128]{0:T(128)} %param.19) | copy-start | bytes 1540
  74.5 39.7 %copy-start.8 = (f32[128]{0:T(128)S(1)}, f32[128]{0:T(128)}, u32[]{:S(2)}) copy-start(f32[128]{0:T(128)} %param.18) | copy-start | bytes 1540
Sparse Core Ops, SparseCore 0:
  18.7 45.9 all-gather.3
where the time goes:
time: 122 us
  blocking collectives  51.1 us (42%)
  waiting for transfers between devices  43.2 us (35%)
  between operations  13.5 us (11%)
  local copies, waits for them, and re-layouts  9.28 us (8%)
  matrix products  3.2 us (3%)
  other arithmetic  1.35 us (1%)
    all_gather x1, waiting for transfers between devices, per_device(): piece = lax.all_gather(pair, 'row', axis=0, tiled=True)  43.2 us
    psum x1, blocking collectives, per_device(): lax.psum((jnp.sum(pre, axis=0), jnp.sum(pre * pre, axis=0)), ('row', 'rep...  30.5 us
    all_gather x1, blocking collectives, per_device(): pair = lax.all_gather(local_x, 'feat', axis=0, tiled=True)  12 us
    all_gather x1, blocking collectives, per_device(): agg_pair = lax.all_gather(agg, 'feat', axis=0, tiled=True)  8.55 us
    squeeze x4, local copies, waits for them, and re-layouts, one_shard(): shard = lax.dynamic_index_in_dim(shards, step, 0, keepdims=False)  4.32 us
  transfers between devices with their start and end apart: 1, of which 1 were waited for; matrix products, arithmetic and copies ran while one was open for 2% of the time, Pallas kernels for 0%

commit v1 on v0

--- a/solution.py
+++ b/solution.py
@@ -41,9 +41,8 @@
     pre = jnp.dot(pair, w_self, preferred_element_type=jnp.float32) + jnp.dot(
         agg_pair, w_neigh, preferred_element_type=jnp.float32
     )
-    col_sum, col_sq = lax.psum(
-        (jnp.sum(pre, axis=0), jnp.sum(pre * pre, axis=0)), ("row", "replica")
-    )
+    pipes_handle = lambda sample: jax.lax.psum(jax.lax.psum(sample, "row"), "replica")
+    col_sum, col_sq = pipes_handle((jnp.sum(pre, axis=0), jnp.sum(pre * pre, axis=0)))
     total_nodes = pre.shape[0] * lax.axis_size("row") * lax.axis_size("replica")
     mean = col_sum / total_nodes
     var = col_sq / total_nodes - mean * mean

time: 122 us -> 107 us (0.88)
  blocking collectives: 51.1 us -> 36.3 us
    psum x1 -> x2, blocking collectives: 30.5 us -> 15.7 us  [the longest x1 10.1 us: per_device(): jax.lax.psum(sample, 'row')]
  transfers between devices with their start and end apart: 1 -> 1, of which waited for: 1 -> 1; matrix products, arithmetic and copies ran while one was open for 2% -> 3% of each run, Pallas kernels for 0% -> 0%
where the time goes in v1:
time: 107 us
  waiting for transfers between devices  43.2 us (40%)
  blocking collectives  36.3 us (34%)
  between operations  13.5 us (13%)
  local copies, waits for them, and re-layouts  9.28 us (9%)
  matrix products  3.2 us (3%)
  other arithmetic  1.35 us (1%)
    all_gather x1, waiting for transfers between devices, per_device(): piece = lax.all_gather(pair, 'row', axis=0, tiled=True)  43.2 us
    all_gather x1, blocking collectives, per_device(): pair = lax.all_gather(local_x, 'feat', axis=0, tiled=True)  12 us
    psum x1, blocking collectives, per_device(): jax.lax.psum(sample, 'row')  10.1 us
    all_gather x1, blocking collectives, per_device(): agg_pair = lax.all_gather(agg, 'feat', axis=0, tiled=True)  8.54 us
    psum x1, blocking collectives, per_device(): jax.lax.psum(jax.lax.psum(sample, 'row'), 'replica')  5.65 us
    squeeze x4, local copies, waits for them, and re-layouts, one_shard(): shard = lax.dynamic_index_in_dim(shards, step, 0, keepdims=False)  4.32 us
    gather x4, local copies, waits for them, and re-layouts, one_shard(): picked = shard[cols_now]  2.39 us
  transfers between devices with their start and end apart: 1, of which 1 were waited for; matrix products, arithmetic and copies ran while one was open for 3% of the time, Pallas kernels for 0%

profile of v1, /device:TPU:0, one launch (start us, length us, event | category | flops | bytes accessed | tf_op | source)
XLA Modules:
  0.0 107.0 jit_solution(4621469488110404667)
XLA Ops:
  6.5 0.0 copy-start
  6.5 0.0 all-gather.4.cloned.1.call-start
  6.5 12.0 %all-gather = bf16[1,1024,256]{2,1,0:T(8,128)(2,1)} all-gather(bf16[1,512,256]{2,1,0:T(8,128)(2,1)} %param.11), channel_id=2, replica_groups=mesh['row'=4,'replica'=4,'feat'=2] {'feat'}, dimensions={1}, use_global_device_ids=true | all-gather | bytes 786432 | tf_op jit(solution)/shard_map/all_gather | solution.py:17
  18.6 0.0 all-gather.4.cloned.1.call-update
  18.6 0.0 copy-start.4
  18.6 0.0 copy-start.5
  18.6 0.0 copy-start.6
  18.6 0.0 copy-start.1
  18.6 0.0 copy-start.3
  18.7 1.6 %copy.20 = bf16[1,4,4,3,128,128]{5,4,3,1,2,0:T(8,128)(2,1)S(1)} copy(bf16[1,4,4,3,128,128]{5,4,3,2,1,0:T(8,128)(2,1)} %param.12) | data formatting | bytes 3145728 | tf_op args[1]
  20.2 0.0 copy-done.4
  20.2 0.1 copy.17
  20.4 0.0 copy-done.5
  20.4 0.1 copy.16
  20.4 0.0 copy-done.6
  20.5 0.0 copy-done.1
  20.5 0.0 copy-done.3
  20.5 1.1 %fusion.10 = f32[1024,128]{1,0:T(8,128)} fusion(bf16[256,128]{1,0:T(8,128)(2,1)S(1)} %copy-done.3, bf16[1,1024,256]{2,1,0:T(8,128)(2,1)S(1)} %copy-done.1), kind=kOutput, calls=%fused_computation.20 | convolution fusion | flops 67108864 | bytes 1114112 | tf_op jit(solution)/shard_map/dot_general | solution.py:41
  21.6 43.2 %all-gather.4.cloned.1.call-done = bf16[1,4096,256]{2,1,0:T(8,128)(2,1)} async-done(((bf16[1,1024,256]{2,1,0:T(8,128)(2,1)}), bf16[1,4096,256]{2,1,0:T(8,128)(2,1)}) %all-gather.4.cloned.1.call-update) | async-done | bytes 2097168 | tf_op jit(solution)/shard_map/all_gather | solution.py:22
  64.7 9.8 %while.14 = (s32[]{:T(128)}, f32[4,128,256]{2,1,0:T(8,128)S(1)}, s32[4,4]{0,1:T(4,128)S(1)}, bf16[4,4,3,128,128]{4,3,2,0,1:T(8,128)(2,1)S(1)}, bf16[4,8,128,256]...) while((s32[]{:T(128)}, f32[4,128,256]{2,1,0:T(8,128)S(1)}, ...), condition=%wide.region_1.2_spmd.clone, body=%wide.region_0.1_spmd.clone.sunk | while | flops 101123120 | bytes 4854827 | solution.py:38
  64.7 1.1 %dynamic-slice_bitcast_fusion.2 = bf16[8,128,256]{2,1,0:T(8,128)(2,1)S(1)} fusion(bf16[4,8,128,256]{3,2,1,0:T(8,128)(2,1)} %get-tuple-element.243, s32[]{:T(128)} %get-tuple-element.231), kind=kLoop, calls=%fused_computation.4.clone.1 | loop fusion | bytes 1048580 | tf_op jit(solution)/shard_map/while/body/eval_jaxpr/jit(dynamic_index_in_dim)/squeeze | solution.py:27
  65.8 0.1 copy.22
  65.9 0.1 reshape.106
  66.0 0.6 gather_fusion
  66.6 0.1 iota_compare_fusion.2
  66.7 0.4 fusion.23
  67.2 1.1 %dynamic-slice_bitcast_fusion.2 = bf16[8,128,256]{2,1,0:T(8,128)(2,1)S(1)} fusion(bf16[4,8,128,256]{3,2,1,0:T(8,128)(2,1)} %get-tuple-element.243, s32[]{:T(128)} %get-tuple-element.231), kind=kLoop, calls=%fused_computation.4.clone.1 | loop fusion | bytes 1048580 | tf_op jit(solution)/shard_map/while/body/eval_jaxpr/jit(dynamic_index_in_dim)/squeeze | solution.py:27
  68.3 0.1 copy.22
  68.4 0.1 reshape.106
  68.5 0.6 gather_fusion
  69.1 0.1 iota_compare_fusion.2
  69.2 0.4 fusion.23
  69.6 1.1 %dynamic-slice_bitcast_fusion.2 = bf16[8,128,256]{2,1,0:T(8,128)(2,1)S(1)} fusion(bf16[4,8,128,256]{3,2,1,0:T(8,128)(2,1)} %get-tuple-element.243, s32[]{:T(128)} %get-tuple-element.231), kind=kLoop, calls=%fused_computation.4.clone.1 | loop fusion | bytes 1048580 | tf_op jit(solution)/shard_map/while/body/eval_jaxpr/jit(dynamic_index_in_dim)/squeeze | solution.py:27
  70.7 0.1 copy.22
  70.8 0.1 reshape.106
  70.9 0.6 gather_fusion
  71.5 0.1 iota_compare_fusion.2
  71.6 0.4 fusion.23
  72.1 1.1 %dynamic-slice_bitcast_fusion.2 = bf16[8,128,256]{2,1,0:T(8,128)(2,1)S(1)} fusion(bf16[4,8,128,256]{3,2,1,0:T(8,128)(2,1)} %get-tuple-element.243, s32[]{:T(128)} %get-tuple-element.231), kind=kLoop, calls=%fused_computation.4.clone.1 | loop fusion | bytes 1048580 | tf_op jit(solution)/shard_map/while/body/eval_jaxpr/jit(dynamic_index_in_dim)/squeeze | solution.py:27
  73.2 0.1 copy.22
  73.2 0.1 reshape.106
  73.3 0.6 gather_fusion
  74.0 0.1 iota_compare_fusion.2
  74.0 0.4 fusion.23
  74.5 0.0 copy-start.2
  74.5 0.0 copy-start.7
  74.5 0.0 copy-start.8
  74.5 0.1 fusion.9
  74.7 8.5 %all_gather.11 = bf16[1024,256]{1,0:T(8,128)(2,1)S(1)} all-gather(bf16[512,256]{1,0:T(8,128)(2,1)S(1)} %fusion.9), channel_id=1, replica_groups=mesh['row'=4,'replica'=4,'feat'=2] {'feat'}, dimensions={0}, use_global_device_ids=true | all-gather | bytes 786432 | tf_op jit(solution)/shard_map/all_gather | solution.py:40
  83.2 0.0 copy-done
  83.2 0.0 copy-done.2
  83.2 0.4 fusion.13
  83.6 10.1 %all-reduce.1 = (f32[128]{0:T(128)S(1)}, f32[128]{0:T(128)S(1)}) all-reduce(f32[128]{0:T(128)S(1)} %get-tuple-element.166, f32[128]{0:T(128)S(1)} %get-tuple-element.165), channel_id=1, replica_groups=mesh['row'=4,'replica'=4,'feat'=2] {'row'}, use_global_device_ids=true, to_apply=%region_6.7 | all-reduce | flops 256 | bytes 2048 | tf_op jit(solution)/shard_map/psum | solution.py:44
  93.7 5.6 %all-reduce = (f32[128]{0:T(128)S(1)}, f32[128]{0:T(128)S(1)}) all-reduce(f32[128]{0:T(128)S(1)} %get-tuple-element.181, f32[128]{0:T(128)S(1)} %get-tuple-element.182), channel_id=1, replica_groups=mesh['row'=4,'replica'=4,'feat'=2] {'replica'}, use_global_device_ids=true, to_apply=%region_7.8 | all-reduce | flops 256 | bytes 2048 | tf_op jit(solution)/shard_map/psum | solution.py:44
  99.3 0.0 copy-done.7
  99.3 0.0 copy-done.8
  99.3 0.8 fusion.12
  (15 shorter events, 0.1 us)
Async XLA Ops:
  6.5 76.7 %copy-start = (bf16[256,128]{1,0:T(8,128)(2,1)S(1)}, bf16[256,128]{1,0:T(8,128)(2,1)}, u32[]{:S(2)}) copy-start(bf16[256,128]{1,0:T(8,128)(2,1)} %param.17) | copy-start | bytes 196612
  6.5 58.2 %all-gather.4.cloned.1.call-start = ((), (), s32[]{:S(2)}) async-start(), calls=%async_computation | async-start | bytes 2621440 | tf_op jit(solution)/shard_map/all_gather | solution.py:22
  18.6 1.6 %copy-start.4 = (s32[1,4,4,3]{2,1,3,0:T(4,128)S(1)}, s32[1,4,4,3]{2,1,3,0:T(4,128)}, u32[]{:S(2)}) copy-start(s32[1,4,4,3]{2,1,3,0:T(4,128)} %param.13) | copy-start | bytes 580
  18.6 1.7 %copy-start.5 = (s32[1,4,4]{2,1,0:T(4,128)S(1)}, s32[1,4,4]{2,1,0:T(4,128)}, u32[]{:S(2)}) copy-start(s32[1,4,4]{2,1,0:T(4,128)} %param.14) | copy-start | bytes 196
  18.6 1.8 %copy-start.6 = (s32[1,512]{1,0:T(1,128)S(1)}, s32[1,512]{1,0:T(1,128)}, u32[]{:S(2)}) copy-start(s32[1,512]{1,0:T(1,128)} %param.15) | copy-start | bytes 6148
  18.6 1.8 %copy-start.1 = (bf16[1,1024,256]{2,1,0:T(8,128)(2,1)S(1)}, bf16[1,1024,256]{2,1,0:T(8,128)(2,1)}, u32[]{:S(2)}) copy-start(bf16[1,1024,256]{2,1,0:T(8,128)(2,1)} %all-gather) | copy-start | bytes 1572868
  18.6 1.8 %copy-start.3 = (bf16[256,128]{1,0:T(8,128)(2,1)S(1)}, bf16[256,128]{1,0:T(8,128)(2,1)}, u32[]{:S(2)}) copy-start(bf16[256,128]{1,0:T(8,128)(2,1)} %param.16) | copy-start | bytes 196612
  74.5 8.7 %copy-start.2 = (f32[1024,128]{1,0:T(8,128)S(1)}, f32[1024,128]{1,0:T(8,128)}, u32[]{:S(2)}) copy-start(f32[1024,128]{1,0:T(8,128)} %fusion.10) | copy-start | bytes 1572868
  74.5 24.8 %copy-start.7 = (f32[128]{0:T(128)S(1)}, f32[128]{0:T(128)}, u32[]{:S(2)}) copy-start(f32[128]{0:T(128)} %param.19) | copy-start | bytes 1540
  74.5 24.8 %copy-start.8 = (f32[128]{0:T(128)S(1)}, f32[128]{0:T(128)}, u32[]{:S(2)}) copy-start(f32[128]{0:T(128)} %param.18) | copy-start | bytes 1540
Sparse Core Ops, SparseCore 0:
  18.7 45.9 all-gather.3
